TPU v7x, 32 devices: a whole 2x2x4 slice. The times are simulated.
32 devices in a mesh: gx: 8 (over y, x, core), gy: 4 (over z).
Axes of the slice: x: 2, y: 2, z: 4, core: 2. Of those that a mesh axis runs over, the one named last changes fastest.
Arguments:
- resid: bfloat16 [128, 16384], P(('gx', 'gy')), may hold values from -6 to 6
- query: bfloat16 [128, 16384], P(('gx', 'gy')), may hold values from -6 to 6
- key_new: bfloat16 [128, 1024], P(('gx', 'gy')), may hold values from -6 to 6
- value_new: bfloat16 [128, 1024], P(('gx', 'gy')), may hold values from -6 to 6
- cache_keys: bfloat16 [128, 128, 1024], P(('gx', 'gy'))
- cache_values: bfloat16 [128, 128, 1024], P(('gx', 'gy')), may hold values from -6 to 6
- lengths: int32 [128], P(('gx', 'gy')), may hold values from 1 to 128, as said below
- norm_gain: bfloat16 [16384], replicated, may hold values from 0.5 to 1.5
- gate_weight: bfloat16 [16384, 26624], P('gx', 'gy'), may hold values from -0.046875 to 0.046875
- up_weight: bfloat16 [16384, 26624], P('gx', 'gy'), may hold values from -0.046875 to 0.046875
- down_weight: bfloat16 [26624, 16384], P('gy', 'gx'), may hold values from -0.0390625 to 0.0390625
Outputs:
- layer_out: bfloat16 [128, 16384], P(('gx', 'gy'))
Inputs may be any that keep to these rules, and one draw needn't show every extreme that they name: `lengths`: some row has all 128 positions live.
All inputs are finite; a program needn't handle non-finite values.
Results may differ from a plain program's by a relative error of at most 0.0057.
Values may be sent and summed in bfloat16 or wider, within the bound.
A program may use at most 192 MiB of HBM per device.

v0:
```python
import jax
import jax.numpy as jnp
from jax import lax
from jax.sharding import PartitionSpec as P

HQ = 128
KV = 8
HD = 128


def attend_row(query, key_new, value_new, cache_keys, cache_values, length):
    scale_factor = HD ** (-0.5)
    span = cache_keys.shape[0]
    heads = query.astype(jnp.float32).reshape(KV, HQ // KV, HD)
    keys = cache_keys.reshape(span, KV, HD)
    values = cache_values.reshape(span, KV, HD)
    knew = key_new.astype(jnp.float32).reshape(KV, HD)
    vnew = value_new.astype(jnp.float32).reshape(KV, HD)
    scores = (
        jnp.einsum(
            "kgd,pkd->kgp",
            query.reshape(KV, HQ // KV, HD),
            keys,
            preferred_element_type=jnp.float32,
        )
        * scale_factor
    )
    places = jnp.arange(span, dtype=jnp.int32)
    scores = jnp.where(places[None, None, :] < length, scores, jnp.float32(-1e30))
    own = jnp.einsum("kgd,kd->kg", heads, knew) * scale_factor
    top = jnp.maximum(jnp.max(scores, axis=-1), own)
    expo = jnp.exp(scores - top[..., None])
    own_expo = jnp.exp(own - top)
    total = jnp.sum(expo, axis=-1) + own_expo
    probs = (expo / total[..., None]).astype(jnp.bfloat16)
    own_prob = (own_expo / total).astype(jnp.bfloat16).astype(jnp.float32)
    mixed = (
        jnp.einsum("kgp,pkd->kgd", probs, values, preferred_element_type=jnp.float32)
        + own_prob[..., None] * vnew[:, None, :]
    )
    return mixed.reshape(HQ * HD)


def on_device(
    resid,
    query,
    key_new,
    value_new,
    cache_keys,
    cache_values,
    lengths,
    norm_gain,
    gate_weight,
    up_weight,
    down_weight,
):
    attended = jax.vmap(attend_row)(query, key_new, value_new, cache_keys, cache_values, lengths)
    mid = (resid.astype(jnp.float32) + attended).astype(jnp.bfloat16)
    midf = mid.astype(jnp.float32)
    inverse = lax.rsqrt(jnp.mean(midf * midf, axis=-1, keepdims=True) + 1e-05)
    normed = (midf * inverse * norm_gain.astype(jnp.float32)).astype(jnp.bfloat16)
    stacked = jnp.stack([mid, normed], axis=1)
    blocks = lax.all_to_all(stacked, "gx", split_axis=2, concat_axis=0, tiled=True)
    gathered = lax.all_gather(blocks, "gy", axis=0, tiled=True)
    mid_rows = gathered[:, 0, :]
    normed_rows = gathered[:, 1, :]
    gate_part = jnp.dot(normed_rows, gate_weight, preferred_element_type=jnp.float32)
    up_part = jnp.dot(normed_rows, up_weight, preferred_element_type=jnp.float32)
    gate, up = lax.psum((gate_part, up_part), "gx")
    act = (jax.nn.silu(gate) * up).astype(jnp.bfloat16)
    block_rows = act.shape[0] // lax.axis_size("gy")
    ffn = lax.psum_scatter(
        jnp.dot(act, down_weight, preferred_element_type=jnp.float32),
        "gy",
        scatter_dimension=0,
        tiled=True,
    )
    own_mid = lax.dynamic_slice_in_dim(mid_rows, lax.axis_index("gy") * block_rows, block_rows, 0)
    finished = (own_mid.astype(jnp.float32) + ffn).astype(jnp.bfloat16)
    return lax.all_to_all(finished, "gx", split_axis=0, concat_axis=1, tiled=True)


def solution(mesh):
    placed = (
        P(("gx", "gy"), None),
        P(("gx", "gy"), None),
        P(("gx", "gy"), None),
        P(("gx", "gy"), None),
        P(("gx", "gy"), None, None),
        P(("gx", "gy"), None, None),
        P(("gx", "gy")),
        P(),
        P("gx", "gy"),
        P("gx", "gy"),
        P("gy", "gx"),
    )
    return jax.shard_map(
        on_device, mesh=mesh, in_specs=placed, out_specs=P(("gx", "gy"), None), check_vma=False
    )
```

profile of v0, /device:TPU:0, one launch (start us, length us, event | category | flops | bytes accessed | tf_op | source)
XLA Modules:
  0.0 320.8 jit_solution(10934704975294698136)
XLA Ops:
  6.5 0.0 copy-start
  6.5 0.0 copy-start.3
  6.5 0.0 all-gather.2.cloned.1.call-start
  6.5 0.8 iota_compare_fusion
  7.4 0.7 reshape.67
  8.1 0.7 convert_bitcast_fusion
  8.8 0.8 convert_element_type.45
  9.5 0.9 copy.32
  10.5 0.2 fusion.23
  10.6 0.0 copy-done
  10.7 0.7 fusion.22
  11.4 0.3 fusion.14
  11.7 1.7 convolution_add_fusion
  13.4 0.0 copy-done.3
  13.4 0.3 fusion.9
  13.7 0.1 fusion.15
  13.9 0.2 pad_maximum_fusion
  14.1 13.1 %copy.25 = bf16[4,2,16384]{0,1,2:T(2,128)(2,1)} copy(bf16[4,2,16384]{2,0,1:T(4,128)(2,1)S(1)} %pad_maximum_fusion) | data formatting | bytes 524288 | tf_op jit(solution)/shard_map/stack | solution.py:62
  27.2 16.2 %reshape.68 = bf16[8,2,8192]{2,1,0:T(2,128)(2,1)S(1)} reshape(bf16[16384,2,4]{2,1,0:T(2,128)(2,1)} %bitcast.58) | data formatting | bytes 524288
  43.4 11.9 %all_to_all.37 = bf16[8,2,8192]{2,1,0:T(2,128)(2,1)S(1)} all-to-all(bf16[8,2,8192]{2,1,0:T(2,128)(2,1)S(1)} %reshape.68), channel_id=1, replica_groups=mesh['gx'=8,'gy'=4] {'gx'}, dimensions={0} | all-to-all | bytes 524288 | tf_op jit(solution)/shard_map/all_to_all | solution.py:63
  55.3 19.1 %reshape.69 = bf16[16384,2,4]{2,1,0:T(2,128)(2,1)} reshape(bf16[8,2,8192]{2,1,0:T(2,128)(2,1)S(1)} %all_to_all.37) | data formatting | bytes 524288
  74.3 19.2 %copy.26 = bf16[4,2,8,2048]{3,0,2,1:T(4,128)(2,1)S(1)} copy(bf16[4,2,8,2048]{0,1,3,2:T(2,128)(2,1)} %bitcast.59) | data formatting | bytes 524288 | tf_op jit(solution)/shard_map/all_to_all | solution.py:63
  93.5 0.8 all_to_all.30
  94.3 0.0 all-gather.2.cloned.1.call-update
  94.3 0.2 all-reduce.3.cloned.1.call-start
  94.5 27.2 %all-gather.2.cloned.1.call-done = bf16[128,2,2048]{2,0,1:T(8,128)(2,1)} async-done(((bf16[32,2,2048]{2,0,1:T(8,128)(2,1)}), bf16[128,2,2048]{2,0,1:T(8,128)(2,1)}) %all-gather.2.cloned.1.call-update) | async-done | bytes 1048592 | tf_op jit(solution)/shard_map/all_gather | solution.py:64
  121.8 0.0 copy-start.2
  121.8 14.5 %fusion.7 = f32[128,6656]{1,0:T(8,128)} fusion(bf16[2048,6656]{1,0:T(8,128)(2,1)} %param.20, bf16[128,2,2048]{2,0,1:T(8,128)(2,1)} %all-gather.2.cloned.1.call-done), kind=kOutput, calls=%fused_computation.11 | convolution fusion | flops 3489660928 | bytes 31195136 | tf_op jit(solution)/shard_map/dot_general | solution.py:68
  136.3 0.0 copy-done.2
  136.3 14.3 %fusion.8 = f32[128,6656]{1,0:T(8,128)} fusion(bf16[2048,6656]{1,0:T(8,128)(2,1)} %param.19, bf16[128,2,2048]{2,0,1:T(8,128)(2,1)S(1)} %copy-done.2), kind=kOutput, calls=%fused_computation.12 | convolution fusion | flops 3489660928 | bytes 31195136 | tf_op jit(solution)/shard_map/dot_general | solution.py:67
  150.6 0.0 all-reduce.3.cloned.1.call-update
  150.6 0.0 reduce-scatter.2.cloned.1.call-start
  150.6 109.8 %all-reduce.3.cloned.1.call-done = (f32[128,6656]{1,0:T(8,128)}, f32[128,6656]{1,0:T(8,128)}) async-done(((f32[128,6656]{1,0:T(8,128)}, f32[128,6656]{1,0:T(8,128)}), (f32[128,6656]{1,0:T(8,128)}, f32[128,6656]{1,0:T(8,128)})) %all-reduce.3.cloned.1.call-update) | async-done | bytes 6815760 | tf_op jit(solution)/shard_map/psum | solution.py:69
  260.4 0.0 slice-start
  260.4 0.0 copy-start.1
  260.4 15.7 %fusion = f32[128,2048]{1,0:T(8,128)} fusion(bf16[6656,2048]{1,0:T(8,128)(2,1)} %param.21, f32[128,6656]{1,0:T(8,128)} %get-tuple-element.5, f32[128,6656]{1,0:T(8,128)} %get-tuple-element.6), kind=kOutput, calls=%fused_computation.1 | convolution fusion | flops 3494772736 | bytes 35127296 | tf_op jit(solution)/shard_map/dot_general | solution.py:73
  276.2 0.0 reduce-scatter.2.cloned.1.call-update
  276.2 27.4 %reduce-scatter.2.cloned.1.call-done = f32[32,2048]{1,0:T(8,128)} async-done(((f32[128,2048]{1,0:T(8,128)}), f32[32,2048]{1,0:T(8,128)}) %reduce-scatter.2.cloned.1.call-update) | async-done | bytes 262160 | tf_op jit(solution)/shard_map/reduce_scatter | solution.py:72
  303.6 0.0 slice-done
  303.6 1.0 fusion.13
  304.6 0.1 all_to_all.31
  304.6 9.0 %all_to_all.38 = bf16[8,4,2048]{2,1,0:T(4,128)(2,1)S(1)} all-to-all(bf16[8,4,2048]{2,1,0:T(4,128)(2,1)S(1)} %all_to_all.31), channel_id=1, replica_groups=mesh['gx'=8,'gy'=4] {'gx'}, dimensions={0} | all-to-all | bytes 262144 | tf_op jit(solution)/shard_map/all_to_all | solution.py:80
  313.6 0.7 copy.52
  314.3 0.0 copy-done.1
  (4 shorter events, 0.0 us)
Async XLA Ops:
  6.5 4.1 %copy-start = (bf16[4,128,1024]{2,1,0:T(8,128)(2,1)S(1)}, bf16[4,128,1024]{2,1,0:T(8,128)(2,1)}, u32[]{:S(2)}) copy-start(bf16[4,128,1024]{2,1,0:T(8,128)(2,1)} %param.15) | copy-start | bytes 3145732
  6.5 6.8 %copy-start.3 = (bf16[4,16384]{1,0:T(4,128)(2,1)S(1)}, bf16[4,16384]{1,0:T(4,128)(2,1)}, u32[]{:S(2)}) copy-start(bf16[4,16384]{1,0:T(4,128)(2,1)} %param.11) | copy-start | bytes 393220
  6.5 115.2 %all-gather.2.cloned.1.call-start = ((), (), s32[]{:S(2)}) async-start(), calls=%async_computation.3 | async-start | bytes 1310720 | tf_op jit(solution)/shard_map/all_gather | solution.py:64
  94.3 166.1 %all-reduce.3.cloned.1.call-start = ((), (), s32[]{:S(2)}) async-start(), calls=%async_computation.5 | async-start | bytes 13631488 | tf_op jit(solution)/shard_map/psum | solution.py:69
  121.8 14.5 %copy-start.2 = (bf16[128,2,2048]{2,0,1:T(8,128)(2,1)S(1)}, bf16[128,2,2048]{2,0,1:T(8,128)(2,1)}, u32[]{:S(2)}) copy-start(bf16[128,2,2048]{2,0,1:T(8,128)(2,1)} %all-gather.2.cloned.1.call-done) | copy-start | bytes 3145732
  150.6 153.0 %reduce-scatter.2.cloned.1.call-start = ((), (), s32[]{:S(2)}) async-start(), calls=%async_computation.4 | async-start | bytes 1310720 | tf_op jit(solution)/shard_map/reduce_scatter | solution.py:72
  260.4 43.2 %slice-start = ((bf16[128,2,2048]{2,0,1:T(8,128)(2,1)}), bf16[128,1,2048]{2,0,1:T(8,128)(2,1)S(1)}, s32[]{:S(2)}) async-start(bf16[128,2,2048]{2,0,1:T(8,128)(2,1)} %all-gather.2.cloned.1.call-done), calls=%async_computation.6 | async-start | bytes 1048576 | tf_op jit(solution)/shard_map/slice | solution.py:65
  260.4 53.9 %copy-start.1 = (bf16[4,128,1024]{2,1,0:T(8,128)(2,1)S(1)}, bf16[4,128,1024]{2,1,0:T(8,128)(2,1)}, u32[]{:S(2)}) copy-start(bf16[4,128,1024]{2,1,0:T(8,128)(2,1)} %param.15) | copy-start | bytes 3145732
Sparse Core Ops, SparseCore 0:
  94.4 27.2 all-gather.1
  150.7 109.6 all-reduce.2
  276.3 27.2 reduce-scatter.1
where the time goes:
time: 322 us; the launch traced here: 321 us
  waiting for transfers between devices  164 us (51%)
  local copies, waits for them, and re-layouts  70.7 us (22%)
  matrix products  47.1 us (15%)
  blocking collectives  20.9 us (6%)
  between operations  13.2 us (4%)
  other arithmetic  4.23 us (1%)
    psum x1, waiting for transfers between devices, on_device(): gate, up = lax.psum((gate_part, up_part), 'gx')  110 us
    unnamed x13, local copies, waits for them, and re-layouts  36.9 us
    reduce_scatter x1, waiting for transfers between devices, on_device(): lax.psum_scatter(jnp.dot(act, down_weight, preferred_element_type=jnp.flo...  27.4 us
    all_gather x1, waiting for transfers between devices, on_device(): gathered = lax.all_gather(blocks, 'gy', axis=0, tiled=True)  27.2 us
    all_to_all x2, local copies, waits for them, and re-layouts, on_device(): lax.all_to_all(stacked, 'gx', split_axis=2, concat_axis=0, tiled=True)  20 us
    dot_general x1, matrix products, on_device(): jnp.dot(act, down_weight, preferred_element_type=jnp.float32)  15.7 us
    dot_general x1, matrix products, on_device(): jnp.dot(normed_rows, up_weight, preferred_element_type=jnp.float32)  14.5 us
    dot_general x1, matrix products, on_device(): jnp.dot(normed_rows, gate_weight, preferred_element_type=jnp.float32)  14.3 us
  transfers between devices with their start and end apart: 3, of which 3 were waited for; matrix products, arithmetic and copies ran while one was open for 0% of the time, Pallas kernels for 0%

commit v1 on v0

--- a/solution.py
+++ b/solution.py
@@ -6,6 +6,22 @@
 HQ = 128
 KV = 8
 HD = 128
+
+
+def swapped_with_each(value, axis, split, join):
+    ways, here = (lax.axis_size(axis), lax.axis_index(axis))
+    width = value.shape[split] // ways
+    shape = list(value.shape)
+    shape[split] = width
+    height = shape[join]
+    shape[join] = height * ways
+    full = jnp.zeros(shape, value.dtype)
+    for mask in range(ways):
+        part = lax.dynamic_slice_in_dim(value, (here ^ mask) * width, width, axis=split)
+        if mask:
+            part = lax.ppermute(part, axis, [(d, d ^ mask) for d in range(ways)])
+        full = lax.dynamic_update_slice_in_dim(full, part, (here ^ mask) * height, axis=join)
+    return full
 
 
 def attend_row(query, key_new, value_new, cache_keys, cache_values, length):
@@ -60,7 +76,7 @@
     inverse = lax.rsqrt(jnp.mean(midf * midf, axis=-1, keepdims=True) + 1e-05)
     normed = (midf * inverse * norm_gain.astype(jnp.float32)).astype(jnp.bfloat16)
     stacked = jnp.stack([mid, normed], axis=1)
-    blocks = lax.all_to_all(stacked, "gx", split_axis=2, concat_axis=0, tiled=True)
+    blocks = swapped_with_each(stacked, "gx", 2, 0)
     gathered = lax.all_gather(blocks, "gy", axis=0, tiled=True)
     mid_rows = gathered[:, 0, :]
     normed_rows = gathered[:, 1, :]

time: 322 us -> 258 us (0.80)
  local copies, waits for them, and re-layouts: 70.7 us -> 3.28 us
  blocking collectives: 20.9 us -> 8.97 us
  waiting for transfers between devices: 164 us -> 172 us
  starting transfers between devices: 0.27 us -> 8.13 us
    unnamed x13, local copies, waits for them, and re-layouts: 36.9 us -> 2.29 us
    all_to_all x2 -> x0, local copies, waits for them, and re-layouts: 20 us -> none  [on_device(): lax.all_to_all(stacked, 'gx', split_axis=2, concat_axis=0, tiled=True)]
    another operation x1 -> x0, local copies, waits for them, and re-layouts: 13.1 us -> none  [on_device(): stacked = jnp.stack([mid, normed], axis=1)]
    all_to_all x1 -> x0, blocking collectives: 11.9 us -> none  [on_device(): lax.all_to_all(stacked, 'gx', split_axis=2, concat_axis=0, tiled=True)]
    ppermute x0 -> x7, starting transfers between devices: none -> 7.86 us  [swapped_with_each(): part = lax.ppermute(part, axis, [(d, d ^ mask) for d in range(ways)])]
    ppermute x0 -> x7, waiting for transfers between devices: none -> 5.58 us  [swapped_with_each(): part = lax.ppermute(part, axis, [(d, d ^ mask) for d in range(ways)])]
  transfers between devices with their start and end apart: 3 -> 10, of which waited for: 3 -> 5; matrix products, arithmetic and copies ran while one was open for 0% -> 0% of each run, Pallas kernels for 0% -> 0%
where the time goes in v1:
time: 258 us; the launch traced here: 257 us
  waiting for transfers between devices  172 us (67%)
  matrix products  47.2 us (18%)
  between operations  13.3 us (5%)
  blocking collectives  8.97 us (3%)
  starting transfers between devices  8.13 us (3%)
  other arithmetic  4.2 us (2%)
  local copies, waits for them, and re-layouts  3.28 us (1%)
    psum x1, waiting for transfers between devices, on_device(): gate, up = lax.psum((gate_part, up_part), 'gx')  110 us
    all_gather x1, waiting for transfers between devices, on_device(): gathered = lax.all_gather(blocks, 'gy', axis=0, tiled=True)  29.4 us
    reduce_scatter x1, waiting for transfers between devices, on_device(): lax.psum_scatter(jnp.dot(act, down_weight, preferred_element_type=jnp.flo...  27.4 us
    dot_general x1, matrix products, on_device(): jnp.dot(act, down_weight, preferred_element_type=jnp.float32)  15.8 us
    dot_general x1, matrix products, on_device(): jnp.dot(normed_rows, up_weight, preferred_element_type=jnp.float32)  14.6 us
    dot_general x1, matrix products, on_device(): jnp.dot(normed_rows, gate_weight, preferred_element_type=jnp.float32)  14.3 us
    all_to_all x1, blocking collectives, on_device(): lax.all_to_all(finished, 'gx', split_axis=0, concat_axis=1, tiled=True)  8.97 us
    ppermute x7, starting transfers between devices, swapped_with_each(): part = lax.ppermute(part, axis, [(d, d ^ mask) for d in range(ways)])  7.86 us
  transfers between devices with their start and end apart: 10, of which 5 were waited for; matrix products, arithmetic and copies ran while one was open for 0% of the time, Pallas kernels for 0%

profile of v1, /device:TPU:0, one launch (start us, length us, event | category | flops | bytes accessed | tf_op | source)
XLA Modules:
  0.0 257.1 jit_solution(97644136628100007)
XLA Ops:
  6.5 0.0 copy-start
  6.5 0.0 all-gather.2.cloned.1.call-start
  6.5 0.8 iota_compare_fusion
  7.4 0.7 reshape.67
  8.1 0.7 convert_bitcast_fusion
  8.8 0.8 convert_element_type.45
  9.5 0.9 copy.19
  10.5 0.2 fusion.32
  10.6 0.0 copy-done
  10.7 0.7 fusion.31
  11.4 0.3 fusion.14
  11.7 1.7 convolution_add_fusion
  13.4 0.0 copy-done.4
  13.4 0.3 fusion.9
  13.7 0.1 fusion.15
  13.9 0.1 fusion.18
  14.0 0.5 collective-permute-start
  14.6 3.6 %collective-permute-start.5 = (bf16[4,2,2048]{2,0,1:T(4,128)(2,1)S(1)}, bf16[4,2,2048]{2,0,1:T(4,128)(2,1)S(1)}, u32[]{:S(2)}, u32[]{:S(2)}) collective-permute-start(bf16[4,2,2048]{2,0,1:T(4,128)(2,1)S(1)} %get-tuple-element.14), channel_id=1, source_target_pairs={{0,24},{4,28},{8,16},{12,20},{16,8},{20,12},{24,0},{28,4},{1,25},{... | collective-permute-start | bytes 98312 | tf_op jit(solution)/shard_map/ppermute | solution.py:22
  18.2 0.5 collective-permute-start.3
  18.7 1.0 collective-permute-start.4
  19.7 0.3 collective-permute-start.6
  20.0 0.0 collective-permute-done
  20.0 1.9 collective-permute-start.1
  21.9 2.2 collective-permute-done.1
  24.1 0.1 collective-permute-start.2
  24.2 3.4 %collective-permute-done.2 = bf16[4,2,2048]{2,0,1:T(4,128)(2,1)S(1)} collective-permute-done((bf16[4,2,2048]{2,0,1:T(4,128)(2,1)S(1)}, bf16[4,2,2048]{2,0,1:T(4,128)(2,1)S(1)}, u32[]{:S(2)}, u32[]{:S(2)}) %collective-permute-start.2) | collective-permute-done | bytes 32800 | tf_op jit(solution)/shard_map/ppermute | solution.py:22
  27.6 0.0 collective-permute-done.3
  27.6 0.0 collective-permute-done.4
  27.7 0.0 collective-permute-done.5
  27.7 0.0 collective-permute-done.6
  27.8 0.0 copy-start.3
  27.8 0.7 copy-done.3
  28.5 0.0 all-gather.2.cloned.1.call-update
  28.5 0.0 all-reduce.3.cloned.1.call-start
  28.6 29.4 %all-gather.2.cloned.1.call-done = bf16[128,2,2048]{2,0,1:T(8,128)(2,1)} async-done(((bf16[32,2,2048]{2,0,1:T(8,128)(2,1)}), bf16[128,2,2048]{2,0,1:T(8,128)(2,1)}) %all-gather.2.cloned.1.call-update) | async-done | bytes 1048592 | tf_op jit(solution)/shard_map/all_gather | solution.py:80
  57.9 14.6 %fusion.7 = f32[128,6656]{1,0:T(8,128)} fusion(bf16[2048,6656]{1,0:T(8,128)(2,1)} %param.20, bf16[128,2,2048]{2,0,1:T(8,128)(2,1)} %all-gather.2.cloned.1.call-done), kind=kOutput, calls=%fused_computation.11 | convolution fusion | flops 3489660928 | bytes 31195136 | tf_op jit(solution)/shard_map/dot_general | solution.py:84
  72.5 14.3 %fusion.8 = f32[128,6656]{1,0:T(8,128)} fusion(bf16[2048,6656]{1,0:T(8,128)(2,1)} %param.19, bf16[128,2,2048]{2,0,1:T(8,128)(2,1)S(1)} %copy-done.2), kind=kOutput, calls=%fused_computation.12 | convolution fusion | flops 3489660928 | bytes 31195136 | tf_op jit(solution)/shard_map/dot_general | solution.py:83
  86.8 0.0 all-reduce.3.cloned.1.call-update
  86.9 0.2 reduce-scatter.2.cloned.1.call-start
  87.1 109.6 %all-reduce.3.cloned.1.call-done = (f32[128,6656]{1,0:T(8,128)}, f32[128,6656]{1,0:T(8,128)}) async-done(((f32[128,6656]{1,0:T(8,128)}, f32[128,6656]{1,0:T(8,128)}), (f32[128,6656]{1,0:T(8,128)}, f32[128,6656]{1,0:T(8,128)})) %all-reduce.3.cloned.1.call-update) | async-done | bytes 6815760 | tf_op jit(solution)/shard_map/psum | solution.py:85
  196.7 15.8 %fusion = f32[128,2048]{1,0:T(8,128)} fusion(bf16[6656,2048]{1,0:T(8,128)(2,1)} %param.21, f32[128,6656]{1,0:T(8,128)} %get-tuple-element.5, f32[128,6656]{1,0:T(8,128)} %get-tuple-element.6), kind=kOutput, calls=%fused_computation.1 | convolution fusion | flops 3494772736 | bytes 35127296 | tf_op jit(solution)/shard_map/dot_general | solution.py:89
  212.5 0.0 reduce-scatter.2.cloned.1.call-update
  212.5 27.4 %reduce-scatter.2.cloned.1.call-done = f32[32,2048]{1,0:T(8,128)} async-done(((f32[128,2048]{1,0:T(8,128)}), f32[32,2048]{1,0:T(8,128)}) %reduce-scatter.2.cloned.1.call-update) | async-done | bytes 262160 | tf_op jit(solution)/shard_map/reduce_scatter | solution.py:88
  239.9 1.0 fusion.13
  240.9 0.1 all_to_all.14
  240.9 9.0 %all_to_all.19 = bf16[8,4,2048]{2,1,0:T(4,128)(2,1)S(1)} all-to-all(bf16[8,4,2048]{2,1,0:T(4,128)(2,1)S(1)} %all_to_all.14), channel_id=1, replica_groups=mesh['gx'=8,'gy'=4] {'gx'}, dimensions={0} | all-to-all | bytes 262144 | tf_op jit(solution)/shard_map/all_to_all | solution.py:96
  249.9 0.7 copy.47
  250.6 0.0 copy-done.1
  (19 shorter events, 0.3 us)
Async XLA Ops:
  6.5 4.1 %copy-start = (bf16[4,128,1024]{2,1,0:T(8,128)(2,1)S(1)}, bf16[4,128,1024]{2,1,0:T(8,128)(2,1)}, u32[]{:S(2)}) copy-start(bf16[4,128,1024]{2,1,0:T(8,128)(2,1)} %param.15) | copy-start | bytes 3145732
  6.5 6.8 %copy-start.4 = (bf16[4,16384]{1,0:T(4,128)(2,1)S(1)}, bf16[4,16384]{1,0:T(4,128)(2,1)}, u32[]{:S(2)}) copy-start(bf16[4,16384]{1,0:T(4,128)(2,1)} %param.11) | copy-start | bytes 393220
  6.5 51.4 %all-gather.2.cloned.1.call-start = ((), (), s32[]{:S(2)}) async-start(), calls=%async_computation.2 | async-start | bytes 1310720 | tf_op jit(solution)/shard_map/all_gather | solution.py:80
  14.0 6.0 %collective-permute-start = (bf16[4,2,2048]{2,0,1:T(4,128)(2,1)S(1)}, bf16[4,2,2048]{2,0,1:T(4,128)(2,1)S(1)}, u32[]{:S(2)}, u32[]{:S(2)}) collective-permute-start(bf16[4,2,2048]{2,0,1:T(4,128)(2,1)S(1)} %get-tuple-element.11), channel_id=1, source_target_pairs={{0,4},{4,0},{8,12},{12,8},{16,20},{20,16},{24,28},{28,24},{1,5},{5... | collective-permute-start | bytes 98312 | tf_op jit(solution)/shard_map/ppermute | solution.py:22
  14.6 13.1 %collective-permute-start.5 = (bf16[4,2,2048]{2,0,1:T(4,128)(2,1)S(1)}, bf16[4,2,2048]{2,0,1:T(4,128)(2,1)S(1)}, u32[]{:S(2)}, u32[]{:S(2)}) collective-permute-start(bf16[4,2,2048]{2,0,1:T(4,128)(2,1)S(1)} %get-tuple-element.14), channel_id=1, source_target_pairs={{0,24},{4,28},{8,16},{12,20},{16,8},{20,12},{24,0},{28,4},{1,25},{... | collective-permute-start | bytes 98312 | tf_op jit(solution)/shard_map/ppermute | solution.py:22
  18.2 9.4 %collective-permute-start.3 = (bf16[4,2,2048]{2,0,1:T(4,128)(2,1)S(1)}, bf16[4,2,2048]{2,0,1:T(4,128)(2,1)S(1)}, u32[]{:S(2)}, u32[]{:S(2)}) collective-permute-start(bf16[4,2,2048]{2,0,1:T(4,128)(2,1)S(1)} %get-tuple-element.15), channel_id=1, source_target_pairs={{0,16},{4,20},{8,24},{12,28},{16,0},{20,4},{24,8},{28,12},{1,17},{... | collective-permute-start | bytes 98312 | tf_op jit(solution)/shard_map/ppermute | solution.py:22
  18.7 9.0 %collective-permute-start.4 = (bf16[4,2,2048]{2,0,1:T(4,128)(2,1)S(1)}, bf16[4,2,2048]{2,0,1:T(4,128)(2,1)S(1)}, u32[]{:S(2)}, u32[]{:S(2)}) collective-permute-start(bf16[4,2,2048]{2,0,1:T(4,128)(2,1)S(1)} %get-tuple-element.16), channel_id=1, source_target_pairs={{0,20},{4,16},{8,28},{12,24},{16,4},{20,0},{24,12},{28,8},{1,21},{... | collective-permute-start | bytes 98312 | tf_op jit(solution)/shard_map/ppermute | solution.py:22
  19.7 8.1 %collective-permute-start.6 = (bf16[4,2,2048]{2,0,1:T(4,128)(2,1)S(1)}, bf16[4,2,2048]{2,0,1:T(4,128)(2,1)S(1)}, u32[]{:S(2)}, u32[]{:S(2)}) collective-permute-start(bf16[4,2,2048]{2,0,1:T(4,128)(2,1)S(1)} %get-tuple-element.9), channel_id=1, source_target_pairs={{0,28},{4,24},{8,20},{12,16},{16,12},{20,8},{24,4},{28,0},{1,29},{... | collective-permute-start | bytes 98312 | tf_op jit(solution)/shard_map/ppermute | solution.py:22
  20.0 4.1 %collective-permute-start.1 = (bf16[4,2,2048]{2,0,1:T(4,128)(2,1)S(1)}, bf16[4,2,2048]{2,0,1:T(4,128)(2,1)S(1)}, u32[]{:S(2)}, u32[]{:S(2)}) collective-permute-start(bf16[4,2,2048]{2,0,1:T(4,128)(2,1)S(1)} %get-tuple-element.12), channel_id=1, source_target_pairs={{0,8},{4,12},{8,0},{12,4},{16,24},{20,28},{24,16},{28,20},{1,9},{5... | collective-permute-start | bytes 98312 | tf_op jit(solution)/shard_map/ppermute | solution.py:22
  24.1 3.5 %collective-permute-start.2 = (bf16[4,2,2048]{2,0,1:T(4,128)(2,1)S(1)}, bf16[4,2,2048]{2,0,1:T(4,128)(2,1)S(1)}, u32[]{:S(2)}, u32[]{:S(2)}) collective-permute-start(bf16[4,2,2048]{2,0,1:T(4,128)(2,1)S(1)} %get-tuple-element.13), channel_id=1, source_target_pairs={{0,12},{4,8},{8,4},{12,0},{16,28},{20,24},{24,20},{28,16},{1,13},{... | collective-permute-start | bytes 98312 | tf_op jit(solution)/shard_map/ppermute | solution.py:22
  27.8 0.7 copy-start.3
  28.5 168.2 %all-reduce.3.cloned.1.call-start = ((), (), s32[]{:S(2)}) async-start(), calls=%async_computation.4 | async-start | bytes 13631488 | tf_op jit(solution)/shard_map/psum | solution.py:85
  57.9 14.6 %copy-start.2 = (bf16[128,2,2048]{2,0,1:T(8,128)(2,1)S(1)}, bf16[128,2,2048]{2,0,1:T(8,128)(2,1)}, u32[]{:S(2)}) copy-start(bf16[128,2,2048]{2,0,1:T(8,128)(2,1)} %all-gather.2.cloned.1.call-done) | copy-start | bytes 3145732
  86.9 153.0 %reduce-scatter.2.cloned.1.call-start = ((), (), s32[]{:S(2)}) async-start(), calls=%async_computation.3 | async-start | bytes 1310720 | tf_op jit(solution)/shard_map/reduce_scatter | solution.py:88
  196.7 43.2 %slice-start = ((bf16[128,2,2048]{2,0,1:T(8,128)(2,1)}), bf16[128,1,2048]{2,0,1:T(8,128)(2,1)S(1)}, s32[]{:S(2)}) async-start(bf16[128,2,2048]{2,0,1:T(8,128)(2,1)} %all-gather.2.cloned.1.call-done), calls=%async_computation.5 | async-start | bytes 1048576 | tf_op jit(solution)/shard_map/slice | solution.py:81
  196.7 53.9 %copy-start.1 = (bf16[4,128,1024]{2,1,0:T(8,128)(2,1)S(1)}, bf16[4,128,1024]{2,1,0:T(8,128)(2,1)}, u32[]{:S(2)}) copy-start(bf16[4,128,1024]{2,1,0:T(8,128)(2,1)} %param.15) | copy-start | bytes 3145732
Sparse Core Ops, SparseCore 0:
  28.6 29.2 all-gather.1
  87.0 109.6 all-reduce.2
  212.6 27.2 reduce-scatter.1
